TPU v7x, 32 devices: a whole 2x2x4 slice. The times are simulated.
32 devices in a mesh: grid: 4 (over y, x), band: 8 (over z, core).
Axes of the slice: x: 2, y: 2, z: 4, core: 2. Of those that a mesh axis runs over, the one named last changes fastest.
Arguments:
- orbitals: float32 [160, 16, 64, 128], P('band', 'grid'), may hold values from -6 to 6
- occupation: float32 [160], P('band'), may hold values from 0.00625 to 0.05
- core_density: float32 [16, 64, 128], P('grid'), may hold values from 0.2 to 2
- local_potential: float32 [16, 64, 128], P('grid'), may hold values from -6 to 6
Outputs:
- applied: float32 [160, 16, 64, 128], P('band', 'grid')
All inputs are finite; a program needn't handle non-finite values.
Results may differ from a plain program's by a relative error of at most 0.0001.
Values sent between devices are 32-bit elements; how exact they have to be, the bound alone decides.
A program may use at most 192 MiB of HBM per device.

v0:
```python
import jax
import jax.numpy as jnp
from jax import lax
from jax.sharding import PartitionSpec as P


def with_halo(cells, sides, width):
    for axis, dim in sides:
        count = lax.axis_size(axis)
        head = lax.slice_in_dim(cells, 0, width, axis=dim)
        tail = lax.slice_in_dim(cells, cells.shape[dim] - width, cells.shape[dim], axis=dim)
        cells = jnp.concatenate(
            [
                lax.ppermute(tail, axis, [(i, (i + 1) % count) for i in range(count)]),
                cells,
                lax.ppermute(head, axis, [((i + 1) % count, i) for i in range(count)]),
            ],
            axis=dim,
        )
    return cells


def derive_roll(field, axis):
    ahead = jnp.roll(field, -1, axis) - jnp.roll(field, 1, axis)
    far = jnp.roll(field, -2, axis) - jnp.roll(field, 2, axis)
    return (8.0 * ahead - far) / 12.0


def derive_padded(padded, count, axis):

    def part(lower, upper):
        return lax.slice_in_dim(padded, lower, upper, 1, axis)

    ahead = part(3, count + 3) - part(1, count + 1)
    far = part(4, count + 4) - part(0, count)
    return (8.0 * ahead - far) / 12.0


def pointwise(density, kinetic, local_potential):
    uniform = 2.871 * jnp.power(density, 5.0 / 3.0)
    ratio = kinetic / (kinetic + uniform)
    potential = local_potential - 0.7386 * jnp.power(density, 1.0 / 3.0) * (1.0 + 0.3 * ratio)
    weight = 1.0 + 0.4 * ratio
    return (potential, weight)


def per_device(orbitals, occupation, core_density, local_potential):
    cells = orbitals.shape[1]
    padded = with_halo(orbitals, (("grid", 1),), 2)
    extra = 0
    span = cells + 2 * extra
    grad_x = derive_padded(padded, span, 1)
    inner = padded[:, 2 : 2 + span]
    grad_y = derive_roll(inner, 2)
    grad_z = derive_roll(inner, 3)
    occ4 = occupation[:, None, None, None]
    rho_part = jnp.sum(occ4 * orbitals * orbitals, axis=0)
    tau_part = 0.5 * jnp.sum(occ4 * (grad_x * grad_x + grad_y * grad_y + grad_z * grad_z), axis=0)
    rho_sum, tau_sum = lax.psum((rho_part, tau_part), "band")
    potential, weight = pointwise(core_density + rho_sum, tau_sum, local_potential)
    flux_x = weight[None] * grad_x
    flux_padded = with_halo(flux_x, (("grid", 1),), 2)
    div_x = derive_padded(flux_padded, cells, 1)
    div_y = derive_roll(weight[None] * grad_y, 2)
    div_z = derive_roll(weight[None] * grad_z, 3)
    return -0.5 * (div_x + div_y + div_z) + potential[None] * orbitals


def solution(mesh):
    in_specs = (
        P("band", "grid", None, None),
        P("band"),
        P("grid", None, None),
        P("grid", None, None),
    )
    out_specs = P("band", "grid", None, None)
    return jax.shard_map(
        per_device, mesh=mesh, in_specs=in_specs, out_specs=out_specs, check_vma=False
    )
```

profile of v0, /device:TPU:0, one launch (start us, length us, event | category | flops | bytes accessed | tf_op | source)
XLA Modules:
  0.0 249.7 jit_solution(8585114032396784326)
XLA Ops:
  6.5 2.2 fusion.33
  8.7 4.0 %collective-permute-start = (f32[20,2,64,128]{3,2,1,0:T(8,128)S(1)}, f32[20,2,64,128]{3,2,1,0:T(8,128)S(1)}, u32[]{:S(2)}, u32[]{:S(2)}) collective-permute-start(f32[20,2,64,128]{3,2,1,0:T(8,128)S(1)} %get-tuple-element.30), channel_id=1, source_target_pairs={{8,0},{16,8},{24,16},{0,24},{9,1},{17,9},{25,17},{1,25},{10,2},{18... | collective-permute-start | bytes 3932168 | tf_op jit(solution)/shard_map/ppermute | solution.py:16
  12.7 3.0 %fusion.40 = (f32[20,4,62,128]{3,2,1,0:T(8,128)}, f32[20,4,62,128]{3,2,1,0:T(8,128)}) fusion(f32[20,4,64,128]{3,2,1,0:T(8,128)S(1)} %copy-done), kind=kLoop, calls=%fused_computation.66 | loop fusion | bytes 10158080 | tf_op jit(solution)/shard_map/jit(_roll_static)/slice | solution.py:25
  15.7 3.5 %fusion.34 = (f32[20,4,64,127]{3,2,1,0:T(8,128)}, f32[20,4,64,127]{3,2,1,0:T(8,128)}) fusion(f32[20,4,64,128]{3,2,1,0:T(8,128)S(1)} %copy-done), kind=kLoop, calls=%fused_computation.60 | loop fusion | bytes 10403840 | tf_op jit(solution)/shard_map/jit(_roll_static)/slice | solution.py:24
  19.1 3.3 %fusion.36 = (f32[20,4,64,126]{3,2,1,0:T(8,128)}, f32[20,4,64,126]{3,2,1,0:T(8,128)}) fusion(f32[20,4,64,128]{3,2,1,0:T(8,128)S(1)} %copy-done), kind=kLoop, calls=%fused_computation.62 | loop fusion | bytes 10321920 | tf_op jit(solution)/shard_map/jit(_roll_static)/slice | solution.py:25
  22.5 3.0 %fusion.38 = (f32[20,4,63,128]{3,2,1,0:T(8,128)}, f32[20,4,63,128]{3,2,1,0:T(8,128)}) fusion(f32[20,4,64,128]{3,2,1,0:T(8,128)S(1)} %copy-done), kind=kLoop, calls=%fused_computation.64 | loop fusion | bytes 10321920 | tf_op jit(solution)/shard_map/jit(_roll_static)/slice | solution.py:24
  25.5 0.1 fusion.41
  25.5 0.1 fusion.39
  25.6 3.5 %fusion.37 = (f32[20,4,64,2]{3,2,1,0:T(8,128)}, f32[20,4,64,2]{3,2,1,0:T(8,128)}) fusion(f32[20,4,64,128]{3,2,1,0:T(8,128)S(1)} %copy-done), kind=kLoop, calls=%fused_computation.63 | loop fusion | bytes 163840 | tf_op jit(solution)/shard_map/jit(_roll_static)/slice | solution.py:25
  29.1 3.4 %fusion.35 = (f32[20,4,64,1]{3,2,1,0:T(8,128)}, f32[20,4,64,1]{3,2,1,0:T(8,128)}) fusion(f32[20,4,64,128]{3,2,1,0:T(8,128)S(1)} %copy-done), kind=kLoop, calls=%fused_computation.61 | loop fusion | bytes 81920 | tf_op jit(solution)/shard_map/jit(_roll_static)/slice | solution.py:24
  32.5 37.3 %collective-permute-done.1 = f32[20,2,64,128]{3,2,1,0:T(8,128)S(1)} collective-permute-done((f32[20,2,64,128]{3,2,1,0:T(8,128)S(1)}, f32[20,2,64,128]{3,2,1,0:T(8,128)S(1)}, u32[]{:S(2)}, u32[]{:S(2)}) %collective-permute-start.1) | collective-permute-done | bytes 1310752 | tf_op jit(solution)/shard_map/ppermute | solution.py:14
  69.8 1.2 constant_dynamic-update-slice_fusion.3
  71.0 3.0 %constant_dynamic-update-slice_fusion.1 = (f32[20,6,64,128]{3,2,1,0:T(8,128)}, f32[20,6,64,128]{3,2,1,0:T(8,128)}) fusion(f32[20,4,64,128]{3,2,1,0:T(8,128)S(1)} %copy-done, f32[20,6,64,128]{3,2,1,0:T(8,128)} %constant_dynamic-update-slice_fusion.3), kind=kLoop, calls=%fused_computation.47 | loop fusion | bytes 7864320
  74.0 1.2 constant_dynamic-update-slice_fusion
  75.2 19.9 %fusion = (f32[4,64,128]{2,1,0:T(8,128)}, f32[4,64,128]{2,1,0:T(8,128)S(1)}, f32[20,4,64,128]{3,2,1,0:T(8,128)}, f32[20,4,64,128]{3,2,1,0:T(8,128)}, f32[20,4,64,128]{3,2,1,0:T(8,128)}) fusion(f32[20,4,64,128]{3,2,1,0:T(8,128)S(1)} %copy-done, f32[20]{0:T(128)S(1)} %copy-done.4, f32[20,4,62,128]{3,2,1,0:T(8,128)} %get-tuple-element.47, ...), kind=kLoop, calls=%fused_computation.5 | loop fusion | flops 21561344 | bytes 42205264 | tf_op jit(solution)/shard_map/reduce_sum | solution.py:57
  95.1 0.7 broadcast_multiply_fusion.3
  95.8 56.0 %all-reduce.3.cloned.1.call-done = (f32[4,64,128]{2,1,0:T(8,128)}, f32[4,64,128]{2,1,0:T(8,128)}) async-done(((f32[4,64,128]{2,1,0:T(8,128)}, f32[4,64,128]{2,1,0:T(8,128)}), (f32[4,64,128]{2,1,0:T(8,128)}, f32[4,64,128]{2,1,0:T(8,128)})) %all-reduce.3.cloned.1.call-update) | async-done | bytes 262160 | tf_op jit(solution)/shard_map/psum | solution.py:59
  151.8 1.2 multiply_subtract_fusion
  153.0 4.3 %broadcast_multiply_fusion = (f32[20,4,64,128]{3,2,1,0:T(8,128)S(1)}, f32[20,4,64,128]{3,2,1,0:T(8,128)S(1)}, f32[20,4,64,128]{3,2,1,0:T(8,128)S(1)}) fusion(f32[20,4,64,128]{3,2,1,0:T(8,128)} %get-tuple-element.10, f32[4,64,128]{2,1,0:T(8,128)S(1)} %get-tuple-element.51, f32[20,4,64,128]{3,2,1,0:T(8,128)} %get-tuple-element.9, ...), kind=kLoop, calls=%fused_computation.39 | loop fusion | flops 1966080 | bytes 15859712 | tf_op jit(solution)/shard_map/mul | solution.py:65
  157.3 3.4 %fusion.27 = (f32[20,4,64,127]{3,2,1,0:T(8,128)}, f32[20,4,64,127]{3,2,1,0:T(8,128)}) fusion(f32[20,4,64,128]{3,2,1,0:T(8,128)S(1)} %get-tuple-element.52), kind=kLoop, calls=%fused_computation.53 | loop fusion | bytes 10403840 | tf_op jit(solution)/shard_map/jit(_roll_static)/slice | solution.py:24
  160.7 3.3 %fusion.26 = (f32[20,4,64,1]{3,2,1,0:T(8,128)}, f32[20,4,64,1]{3,2,1,0:T(8,128)}) fusion(f32[20,4,64,128]{3,2,1,0:T(8,128)S(1)} %get-tuple-element.52), kind=kLoop, calls=%fused_computation.52 | loop fusion | bytes 81920 | tf_op jit(solution)/shard_map/jit(_roll_static)/slice | solution.py:24
  164.0 3.4 %fusion.25 = (f32[20,4,64,126]{3,2,1,0:T(8,128)}, f32[20,4,64,126]{3,2,1,0:T(8,128)}) fusion(f32[20,4,64,128]{3,2,1,0:T(8,128)S(1)} %get-tuple-element.52), kind=kLoop, calls=%fused_computation.51 | loop fusion | bytes 10321920 | tf_op jit(solution)/shard_map/jit(_roll_static)/slice | solution.py:25
  167.4 0.1 fusion.28
  167.5 0.3 fusion.32
  167.8 2.4 collective-permute-start.2
  170.2 0.1 fusion.30
  170.3 3.4 %fusion.24 = (f32[20,4,64,2]{3,2,1,0:T(8,128)}, f32[20,4,64,2]{3,2,1,0:T(8,128)}) fusion(f32[20,4,64,128]{3,2,1,0:T(8,128)S(1)} %get-tuple-element.52), kind=kLoop, calls=%fused_computation.50 | loop fusion | bytes 163840 | tf_op jit(solution)/shard_map/jit(_roll_static)/slice | solution.py:25
  173.6 2.8 %fusion.31 = (f32[20,4,63,128]{3,2,1,0:T(8,128)}, f32[20,4,63,128]{3,2,1,0:T(8,128)}) fusion(f32[20,4,64,128]{3,2,1,0:T(8,128)S(1)} %get-tuple-element.53), kind=kLoop, calls=%fused_computation.57 | loop fusion | bytes 10321920 | tf_op jit(solution)/shard_map/jit(_roll_static)/slice | solution.py:24
  176.5 2.9 %fusion.29 = (f32[20,4,62,128]{3,2,1,0:T(8,128)}, f32[20,4,62,128]{3,2,1,0:T(8,128)}) fusion(f32[20,4,64,128]{3,2,1,0:T(8,128)S(1)} %get-tuple-element.53), kind=kLoop, calls=%fused_computation.55 | loop fusion | bytes 10158080 | tf_op jit(solution)/shard_map/jit(_roll_static)/slice | solution.py:25
  179.4 20.2 %collective-permute-done.2 = f32[20,2,64,128]{3,2,1,0:T(8,128)} collective-permute-done((f32[20,2,64,128]{3,2,1,0:T(8,128)S(1)}, f32[20,2,64,128]{3,2,1,0:T(8,128)}, u32[]{:S(2)}, u32[]{:S(2)}) %collective-permute-start.2) | collective-permute-done | bytes 1310752 | tf_op jit(solution)/shard_map/ppermute | solution.py:16
  199.6 26.1 %collective-permute-done.3 = f32[20,2,64,128]{3,2,1,0:T(8,128)} collective-permute-done((f32[20,2,64,128]{3,2,1,0:T(8,128)S(1)}, f32[20,2,64,128]{3,2,1,0:T(8,128)}, u32[]{:S(2)}, u32[]{:S(2)}) %collective-permute-start.3) | collective-permute-done | bytes 1310752 | tf_op jit(solution)/shard_map/ppermute | solution.py:14
  225.7 17.1 %fusion.8 = f32[20,4,64,128]{3,2,1,0:T(8,128)} fusion(f32[20,2,64,128]{3,2,1,0:T(8,128)} %collective-permute-done.3, f32[20,4,64,128]{3,2,1,0:T(8,128)} %copy-done.1, f32[20,2,64,128]{3,2,1,0:T(8,128)} %collective-permute-done.2, f32[20,4,1,128]{3,2,1,0:T(1,128)S(1)} %get-tuple-element.25, f32[20,4,63,128]{3,2,1,0:T(8,128)} %get-tuple-element.27, ...), kind=kLoop, calls=%fused_computation.13 | loop fusion | flops 19005440 | bytes 31588352 | tf_op jit(solution)/shard_map/add | solution.py:66
  (15 shorter events, 0.0 us)
Async XLA Ops:
  6.5 6.2 %copy-start = (f32[20,4,64,128]{3,2,1,0:T(8,128)S(1)}, f32[20,4,64,128]{3,2,1,0:T(8,128)}, u32[]{:S(2)}) copy-start(f32[20,4,64,128]{3,2,1,0:T(8,128)} %param.4) | copy-start | bytes 7864324
  6.5 145.2 %all-reduce.3.cloned.1.call-start = ((), (), s32[]{:S(2)}) async-start(), calls=%async_computation | async-start | bytes 524288 | tf_op jit(solution)/shard_map/psum | solution.py:59
  8.7 65.3 %collective-permute-start = (f32[20,2,64,128]{3,2,1,0:T(8,128)S(1)}, f32[20,2,64,128]{3,2,1,0:T(8,128)S(1)}, u32[]{:S(2)}, u32[]{:S(2)}) collective-permute-start(f32[20,2,64,128]{3,2,1,0:T(8,128)S(1)} %get-tuple-element.30), channel_id=1, source_target_pairs={{8,0},{16,8},{24,16},{0,24},{9,1},{17,9},{25,17},{1,25},{10,2},{18... | collective-permute-start | bytes 3932168 | tf_op jit(solution)/shard_map/ppermute | solution.py:16
  12.7 57.1 %collective-permute-start.1 = (f32[20,2,64,128]{3,2,1,0:T(8,128)S(1)}, f32[20,2,64,128]{3,2,1,0:T(8,128)S(1)}, u32[]{:S(2)}, u32[]{:S(2)}) collective-permute-start(f32[20,2,64,128]{3,2,1,0:T(8,128)S(1)} %get-tuple-element.31), channel_id=1, source_target_pairs={{0,8},{8,16},{16,24},{24,0},{1,9},{9,17},{17,25},{25,1},{2,10},{10... | collective-permute-start | bytes 3932168 | tf_op jit(solution)/shard_map/ppermute | solution.py:14
  74.0 1.2 copy-start.4
  75.2 76.5 %copy-start.2 = (f32[4,64,128]{2,1,0:T(8,128)S(1)}, f32[4,64,128]{2,1,0:T(8,128)}, u32[]{:S(2)}) copy-start(f32[4,64,128]{2,1,0:T(8,128)} %param.7) | copy-start | bytes 393220
  75.2 76.5 %copy-start.3 = (f32[4,64,128]{2,1,0:T(8,128)S(1)}, f32[4,64,128]{2,1,0:T(8,128)}, u32[]{:S(2)}) copy-start(f32[4,64,128]{2,1,0:T(8,128)} %param.6) | copy-start | bytes 393220
  157.3 10.2 %copy-start.1 = (f32[20,4,64,128]{3,2,1,0:T(8,128)}, f32[20,4,64,128]{3,2,1,0:T(8,128)S(1)}, u32[]{:S(2)}) copy-start(f32[20,4,64,128]{3,2,1,0:T(8,128)S(1)} %get-tuple-element.54) | copy-start | bytes 7864324
  167.8 31.8 %collective-permute-start.2 = (f32[20,2,64,128]{3,2,1,0:T(8,128)S(1)}, f32[20,2,64,128]{3,2,1,0:T(8,128)}, u32[]{:S(2)}, u32[]{:S(2)}) collective-permute-start(f32[20,2,64,128]{3,2,1,0:T(8,128)S(1)} %get-tuple-element.28), channel_id=1, source_target_pairs={{8,0},{16,8},{24,16},{0,24},{9,1},{17,9},{25,17},{1,25},{10,2},{18... | collective-permute-start | bytes 3932168 | tf_op jit(solution)/shard_map/ppermute | solution.py:16
  170.2 55.5 %collective-permute-start.3 = (f32[20,2,64,128]{3,2,1,0:T(8,128)S(1)}, f32[20,2,64,128]{3,2,1,0:T(8,128)}, u32[]{:S(2)}, u32[]{:S(2)}) collective-permute-start(f32[20,2,64,128]{3,2,1,0:T(8,128)S(1)} %get-tuple-element.29), channel_id=1, source_target_pairs={{0,8},{8,16},{16,24},{24,0},{1,9},{9,17},{17,25},{25,1},{2,10},{10... | collective-permute-start | bytes 3932168 | tf_op jit(solution)/shard_map/ppermute | solution.py:14
Sparse Core Ops, SparseCore 0:
  95.9 55.7 all-reduce.2
where the time goes:
time: 250 us
  waiting for transfers between devices  140 us (56%)
  local copies, waits for them, and re-layouts  47 us (19%)
  other arithmetic  43.2 us (17%)
  between operations  13.5 us (5%)
  starting transfers between devices  6.41 us (3%)
    ppermute x2, waiting for transfers between devices, with_halo(): lax.ppermute(tail, axis, [(i, (i + 1) % count) for i in range(count)])  63.4 us
    psum x1, waiting for transfers between devices, per_device(): rho_sum, tau_sum = lax.psum((rho_part, tau_part), 'band')  56 us
    ppermute x2, waiting for transfers between devices, with_halo(): lax.ppermute(head, axis, [((i + 1) % count, i) for i in range(count)])  20.2 us
    reduce_sum x1, other arithmetic, per_device(): rho_part = jnp.sum(occ4 * orbitals * orbitals, axis=0)  19.9 us
    slice x8, local copies, waits for them, and re-layouts, derive_roll(): far = jnp.roll(field, -2, axis) - jnp.roll(field, 2, axis)  19.6 us
    slice x8, local copies, waits for them, and re-layouts, derive_roll(): ahead = jnp.roll(field, -1, axis) - jnp.roll(field, 1, axis)  19.4 us
    add x1, other arithmetic, per_device(): return -0.5 * (div_x + div_y + div_z) + potential[None] * orbitals  17.1 us
    ppermute x2, starting transfers between devices, with_halo(): lax.ppermute(head, axis, [((i + 1) % count, i) for i in range(count)])  6.4 us
  transfers between devices with their start and end apart: 5, of which 4 were waited for; matrix products, arithmetic and copies ran while one was open for 13% of the time, Pallas kernels for 0%

commit v1 on v0

v1 whole, which is shorter than its diff:
```python
import functools

import jax
import jax.numpy as jnp
from jax import lax
from jax.experimental import pallas as pl
from jax.experimental.pallas import tpu as pltpu
from jax.sharding import PartitionSpec as P

MESH = pl.DeviceIdType.MESH
NEAR = 8.0 / 12.0
FAR = 1.0 / 12.0


def derive_lead(f):
    n = f.shape[0]

    def at(s):
        return jnp.concatenate([f[s % n :], f[: s % n]], axis=0)

    return NEAR * (at(1) - at(-1)) - FAR * (at(2) - at(-2))


def derive_tile(f, axis):
    n = f.shape[axis]
    ahead = pltpu.roll(f, n - 1, axis) - pltpu.roll(f, 1, axis)
    far = pltpu.roll(f, n - 2, axis) - pltpu.roll(f, 2, axis)
    return NEAR * ahead - FAR * far


def kernel(G, NB, CH, orb, occ, core, lpot, out,
           F, lt, lr, part, red, wp, lw, wl, dx, ret, gys, gzs,
           fs, fr, fo, ls, lrs, lo, ps, pr, ws, wr, vs, vr, vo, rs, rr, ro):
    bands, nx, ny, nz = orb.shape
    X = nx * G
    R = ny // G
    rc = R // CH
    px = X // NB
    npx = nx // px
    me = lax.axis_index("grid")
    bi = lax.axis_index("band")

    def gpeer(k):
        return lax.rem(me + k, G)

    def bpeer(k):
        return lax.rem(bi + k, NB)

    barrier = pltpu.get_barrier_semaphore()
    for k in range(1, G):
        pl.semaphore_signal(barrier, inc=1, device_id={"grid": gpeer(k)}, device_id_type=MESH)
    for k in range(1, NB):
        pl.semaphore_signal(barrier, inc=1, device_id={"band": bpeer(k)}, device_id_type=MESH)
    pl.semaphore_wait(barrier, G - 1 + NB - 1)

    def rows(dev, c):
        return pl.ds(pl.multiple_of(dev * R + c * rc, 8), rc)

    mine = pl.ds(me * nx, nx)
    sends = []

    def remote(src, dst, s, r, dev):
        copy = pltpu.make_async_remote_copy(
            src_ref=src, dst_ref=dst, send_sem=s, recv_sem=r, device_id=dev, device_id_type=MESH)
        copy.start()
        sends.append(copy)
        return copy

    def local(src, dst, s):
        copy = pltpu.make_async_copy(src, dst, s)
        copy.start()
        return copy

    def spread(c):
        got = [
            remote(orb.at[:, :, rows(gpeer(k), c), :], F.at[c, :, mine], fs.at[c, k], fr.at[c, k], {"grid": gpeer(k)})
            for k in range(1, G)
        ]
        return got, local(orb.at[:, :, rows(me, c), :], F.at[c, :, mine], fo.at[c])

    spreads = [spread(0)]

    first = (bi == 0).astype(jnp.float32)

    def sums_x(x, _):
        def body(b, carry):
            tau, rho = carry
            f = orb[b, x]
            gy = derive_tile(f, 0)
            gz = derive_tile(f, 1)
            gys[b, x] = gy
            gzs[b, x] = gz
            o = occ[b]
            return tau + o * (gy * gy + gz * gz), rho + o * (f * f)

        zero = jnp.zeros((ny, nz), jnp.float32)
        tau, rho = lax.fori_loop(0, bands, body, (zero, zero))
        lt[0, x] = 0.5 * tau
        lt[1, x] = rho + first * core[x]
        return 0

    lax.fori_loop(0, nx, sums_x, 0)

    def all_rows(dev):
        return pl.ds(pl.multiple_of(dev * R, 8), R)

    lgot = [
        remote(lt.at[:, :, all_rows(gpeer(k)), :], lr.at[:, mine], ls.at[k], lrs.at[k], {"grid": gpeer(k)})
        for k in range(1, G)
    ]
    lown = local(lt.at[:, :, all_rows(me), :], lr.at[:, mine], lo)
    for c in range(1, CH):
        spreads.append(spread(c))

    vgot, vown, rgot, rown = [], [], [], []
    for c in range(CH):
        got, own = spreads[c]
        if c == 0:
            lown.wait()
            for copy in lgot:
                copy.wait_recv()
        own.wait()
        for copy in got:
            copy.wait_recv()

        def taux_body(b, acc):
            g = derive_lead(F[c, b])
            return acc + (0.5 * occ[b]) * (g * g)

        taux = lax.fori_loop(0, bands, taux_body, jnp.zeros((X, rc, nz), jnp.float32))
        for j in range(NB):
            part[c, j, 0] = taux[j * px : (j + 1) * px] + lr[0, j * px : (j + 1) * px, c * rc : (c + 1) * rc]
            part[c, j, 1] = lr[1, j * px : (j + 1) * px, c * rc : (c + 1) * rc]
        pgot = [
            remote(part.at[c, bpeer(k)], red.at[c, k], ps.at[c, k], pr.at[c, k], {"band": bpeer(k)})
            for k in range(1, NB)
        ]
        total = part[c, bi]
        for k in range(1, NB):
            pgot[k - 1].wait_recv()
            total = total + red[c, k]
        kinetic = total[0]
        density = total[1]
        third = jnp.exp(jnp.log(density) * (1.0 / 3.0))
        uniform = 2.871 * (density * third * third)
        ratio = kinetic / (kinetic + uniform)
        wp[c, bi, 0] = 1.0 + 0.4 * ratio
        wp[c, bi, 1] = -0.7386 * third * (1.0 + 0.3 * ratio)
        wgot = [
            remote(wp.at[c, bi], wp.at[c, bi], ws.at[c, k], wr.at[c, k], {"band": bpeer(k)})
            for k in range(1, NB)
        ]
        for copy in wgot:
            copy.wait_recv()
        vgot.append([
            remote(wp.at[c, pl.ds(gpeer(k) * npx, npx)], lw.at[c, me], vs.at[c, k], vr.at[c, k], {"grid": gpeer(k)})
            for k in range(1, G)
        ])
        vown.append(local(wp.at[c, pl.ds(me * npx, npx)], lw.at[c, me], vo.at[c]))
        weight = jnp.concatenate([wp[c, j, 0] for j in range(NB)], axis=0)

        def dx_body(b, _):
            dx[c, b] = -0.5 * derive_lead(weight * derive_lead(F[c, b]))
            return 0

        lax.fori_loop(0, bands, dx_body, 0)
        rgot.append([
            remote(dx.at[c, :, pl.ds(gpeer(k) * nx, nx)], ret.at[c, me], rs.at[c, k], rr.at[c, k], {"grid": gpeer(k)})
            for k in range(1, G)
        ])
        rown.append(local(dx.at[c, :, mine], ret.at[c, me], ro.at[c]))

    for c in range(CH):
        vown[c].wait()
        for copy in vgot[c]:
            copy.wait_recv()
        for p in range(G):
            at = p * R + c * rc
            for j in range(npx):
                wl[0, j * px : (j + 1) * px, at : at + rc] = lw[c, p, j, 0]
                wl[1, j * px : (j + 1) * px, at : at + rc] = (
                    lw[c, p, j, 1] + lpot[j * px : (j + 1) * px, at : at + rc]
                )

    def apply_x(x, _):
        w = wl[0, x]
        v = wl[1, x]

        def body(b, _):
            div = derive_tile(w * gys[b, x], 0) + derive_tile(w * gzs[b, x], 1)
            out[b, x] = v * orb[b, x] - 0.5 * div
            return 0

        return lax.fori_loop(0, bands, body, 0)

    lax.fori_loop(0, nx, apply_x, 0)

    for c in range(CH):
        rown[c].wait()
        for copy in rgot[c]:
            copy.wait_recv()

        def add_body(b, _):
            for p in range(G):
                at = p * R + c * rc
                out[b, :, at : at + rc] = out[b, :, at : at + rc] + ret[c, p, b]
            return 0

        lax.fori_loop(0, bands, add_body, 0)
    for copy in sends:
        copy.wait_send()


def per_device(orbitals, occupation, core_density, local_potential):
    G = lax.axis_size("grid")
    NB = lax.axis_size("band")
    bands, nx, ny, nz = orbitals.shape
    X = nx * G
    R = ny // G
    CH = 2 if R % 16 == 0 else 1
    rc = R // CH
    px = X // NB
    npx = nx // px
    f32 = jnp.float32
    dma = pltpu.SemaphoreType.DMA
    vmem = pl.BlockSpec(memory_space=pltpu.VMEM)
    return pl.pallas_call(
        functools.partial(kernel, G, NB, CH),
        out_shape=jax.ShapeDtypeStruct(orbitals.shape, f32),
        in_specs=[vmem, pl.BlockSpec(memory_space=pltpu.SMEM), vmem, vmem],
        out_specs=vmem,
        scratch_shapes=[
            pltpu.VMEM((CH, bands, X, rc, nz), f32),
            pltpu.VMEM((2, nx, ny, nz), f32),
            pltpu.VMEM((2, X, R, nz), f32),
            pltpu.VMEM((CH, NB, 2, px, rc, nz), f32),
            pltpu.VMEM((CH, NB, 2, px, rc, nz), f32),
            pltpu.VMEM((CH, NB, 2, px, rc, nz), f32),
            pltpu.VMEM((CH, G, npx, 2, px, rc, nz), f32),
            pltpu.VMEM((2, nx, ny, nz), f32),
            pltpu.VMEM((CH, bands, X, rc, nz), f32),
            pltpu.VMEM((CH, G, bands, nx, rc, nz), f32),
            pltpu.VMEM((bands, nx, ny, nz), f32),
            pltpu.VMEM((bands, nx, ny, nz), f32),
            dma((CH, G)), dma((CH, G)), dma((CH,)),
            dma((G,)), dma((G,)), dma,
            dma((CH, NB)), dma((CH, NB)),
            dma((CH, NB)), dma((CH, NB)),
            dma((CH, G)), dma((CH, G)), dma((CH,)),
            dma((CH, G)), dma((CH, G)), dma((CH,)),
        ],
        compiler_params=pltpu.CompilerParams(
            collective_id=0, has_side_effects=True, vmem_limit_bytes=60 * 1024 * 1024
        ),
    )(orbitals, occupation, core_density, local_potential)


def solution(mesh):
    in_specs = (
        P("band", "grid", None, None),
        P("band"),
        P("grid", None, None),
        P("grid", None, None),
    )
    out_specs = P("band", "grid", None, None)
    return jax.shard_map(
        per_device, mesh=mesh, in_specs=in_specs, out_specs=out_specs, check_vma=False
    )
```

time: 250 us -> 81.3 us (0.33)
  waiting for transfers between devices: 140 us -> 0 us
  Pallas kernels: 0 us -> 77.5 us
  local copies, waits for them, and re-layouts: 47 us -> 3.56 us
  other arithmetic: 43.2 us -> 0 us
  between operations: 13.5 us -> 0.01 us
  starting transfers between devices: 6.41 us -> 0 us
    ppermute x4 -> x0, waiting for transfers between devices: 83.7 us -> none  [the longest x2 63.4 us: with_halo(): lax.ppermute(tail, axis, [(i, (i + 1) % count) for i in range(count)])]
    pallas_call x0 -> x1, Pallas kernels: none -> 77.5 us  [per_device(): pl.pallas_call(functools.partial(kernel, G, NB, CH), out_shape=jax.ShapeD...]
    psum x1 -> x0, waiting for transfers between devices: 56 us -> none  [per_device(): rho_sum, tau_sum = lax.psum((rho_part, tau_part), 'band')]
    slice x18 -> x0, local copies, waits for them, and re-layouts: 41.5 us -> none  [the longest x8 19.6 us: derive_roll(): far = jnp.roll(field, -2, axis) - jnp.roll(field, 2, axis)]
    reduce_sum x1 -> x0, other arithmetic: 19.9 us -> none  [per_device(): rho_part = jnp.sum(occ4 * orbitals * orbitals, axis=0)]
    add x1 -> x0, other arithmetic: 17.1 us -> none  [per_device(): return -0.5 * (div_x + div_y + div_z) + potential[None] * orbitals]
    ppermute x4 -> x0, starting transfers between devices: 6.41 us -> none  [the longest x2 6.4 us: with_halo(): lax.ppermute(head, axis, [((i + 1) % count, i) for i in range(count)])]
    mul x2 -> x0, other arithmetic: 4.97 us -> none  [the longest x1 4.3 us: per_device(): div_z = derive_roll(weight[None] * grad_z, 3)]
  transfers between devices with their start and end apart: 5 -> 0, of which waited for: 4 -> 0; matrix products, arithmetic and copies ran while one was open for 13% -> 0% of each run, Pallas kernels for 0% -> 0%
where the time goes in v1:
time: 81.3 us; the launch traced here: 81.1 us
  Pallas kernels  77.5 us (95%)
  local copies, waits for them, and re-layouts  3.56 us (4%)
    pallas_call x1, Pallas kernels, per_device(): pl.pallas_call(functools.partial(kernel, G, NB, CH), out_shape=jax.ShapeD...  77.5 us
    unnamed x1, local copies, waits for them, and re-layouts  3.56 us

profile of v1, /device:TPU:0, one launch (start us, length us, event | category | flops | bytes accessed | tf_op | source)
XLA Modules:
  0.0 81.1 jit_solution(16195079005693189673)
XLA Ops:
  0.0 77.5 %shard_map.46 = f32[20,4,64,128]{3,2,1,0:T(8,128)} custom-call(f32[20,4,64,128]{3,2,1,0:T(8,128)} %orb.1, f32[20]{0:T(128)} %occ.1, f32[4,64,128]{2,1,0:T(8,128)} %core.1, f32[4,64,128]{2,1,0:T(8,128)} %lpot.1), custom_call_target="tpu_custom_call" | custom-call | tf_op jit(solution)/shard_map/pallas_call | solution.py:227
  77.6 3.6 %copy.6 = f32[20,4,64,128]{3,2,1,0:T(8,128)} copy(f32[20,4,64,128]{3,2,1,0:T(8,128)} %shard_map.46) | data formatting | bytes 5242880

commit v2 on v1

v2 whole, which is shorter than its diff:
```python
import functools

import jax
import jax.numpy as jnp
from jax import lax
from jax.experimental import pallas as pl
from jax.experimental.pallas import tpu as pltpu
from jax.sharding import PartitionSpec as P

MESH = pl.DeviceIdType.MESH
NEAR = 8.0 / 12.0
FAR = 1.0 / 12.0


def derive_lead(f):
    n = f.shape[0]

    def at(s):
        return jnp.concatenate([f[s % n :], f[: s % n]], axis=0)

    return NEAR * (at(1) - at(-1)) - FAR * (at(2) - at(-2))


def derive_tile(f, axis):
    n = f.shape[axis]
    ahead = pltpu.roll(f, n - 1, axis) - pltpu.roll(f, 1, axis)
    far = pltpu.roll(f, n - 2, axis) - pltpu.roll(f, 2, axis)
    return NEAR * ahead - FAR * far


def partner(i, k, n):
    if n & (n - 1):
        return lax.rem(i + k, n)
    out, bit = 0, 1
    while bit < n:
        digit = lax.rem(lax.div(i, bit), 2)
        out = out + bit * (1 - digit if k & bit else digit)
        bit *= 2
    return out


def kernel(G, NB, CH, orb_hbm, occ_hbm, core_hbm, lpot_hbm, out,
           orb, occ, core, lpot, F, lt, lred, lsum, lyz, part, red, wv, wy, lw, wl, dx, ret, gys, gzs,
           os, fs, fr, fo, ls, lr, ms, mr, ml, ps, pr, ws, wr, vs, vr, vl, us, ur, rs, rr, ro):
    bands, nx, ny, nz = orb.shape
    X = nx * G
    R = ny // G
    rc = R // CH
    px = X // NB
    npx = nx // px
    me = lax.axis_index("grid")
    bi = lax.axis_index("band")
    tg, tb = lax.rem(bi, G), npx * me + lax.div(bi, G)
    sg, sb = lax.div(bi, npx), lax.rem(bi, npx) * G + me
    here = jnp.logical_and(tg == me, tb == bi)
    away = jnp.logical_not(here)

    def gpeer(k):
        return partner(me, k, G)

    def bpeer(k):
        return partner(bi, k, NB)

    barrier = pltpu.get_barrier_semaphore()
    for k in range(1, G):
        pl.semaphore_signal(barrier, inc=1, device_id={"grid": gpeer(k)}, device_id_type=MESH)
    for k in range(1, NB):
        pl.semaphore_signal(barrier, inc=1, device_id={"band": bpeer(k)}, device_id_type=MESH)

    @pl.when(away)
    def _():
        for g, b in ((tg, tb), (sg, sb)):
            pl.semaphore_signal(barrier, inc=1, device_id={"grid": g, "band": b}, device_id_type=MESH)

    sends = []

    def remote(src, dst, s, r, dev):
        copy = pltpu.make_async_remote_copy(
            src_ref=src, dst_ref=dst, send_sem=s, recv_sem=r, device_id=dev, device_id_type=MESH)
        copy.start()
        sends.append(copy)
        return copy

    def local(src, dst, s):
        copy = pltpu.make_async_copy(src, dst, s)
        copy.start()
        return copy

    def moved(src, dst, s, r, l, g, b):
        far = pltpu.make_async_remote_copy(
            src_ref=src, dst_ref=dst, send_sem=s, recv_sem=r, device_id={"grid": g, "band": b},
            device_id_type=MESH)
        near = pltpu.make_async_copy(src, dst, l)
        pl.when(away)(far.start)
        pl.when(here)(near.start)

        def wait():
            pl.when(away)(far.wait)
            pl.when(here)(near.wait)

        return wait

    loads = [
        local(src, dst, os.at[i])
        for i, (src, dst) in enumerate(((orb_hbm, orb), (occ_hbm, occ), (core_hbm, core), (lpot_hbm, lpot)))
    ]
    pl.when(away)(lambda: pl.semaphore_wait(barrier, G - 1 + NB - 1 + 2))
    pl.when(here)(lambda: pl.semaphore_wait(barrier, G - 1 + NB - 1))

    def rows(dev, c):
        return pl.ds(pl.multiple_of(dev * R + c * rc, 8), rc)

    mine = pl.ds(me * nx, nx)

    def spread(c):
        got = [
            remote(orb_hbm.at[:, :, rows(gpeer(k), c), :], F.at[c, :, mine], fs.at[c, k], fr.at[c, k], {"grid": gpeer(k)})
            for k in range(1, G)
        ]
        return got, local(orb_hbm.at[:, :, rows(me, c), :], F.at[c, :, mine], fo.at[c])

    spreads = [spread(0)]
    for copy in loads:
        copy.wait()

    first = (bi == 0).astype(jnp.float32)

    def sums_x(x, _):
        def body(b, carry):
            tau, rho = carry
            f = orb[b, x]
            gy = derive_tile(f, 0)
            gz = derive_tile(f, 1)
            gys[b, x] = gy
            gzs[b, x] = gz
            o = occ[b]
            return tau + o * (gy * gy + gz * gz), rho + o * (f * f)

        zero = jnp.zeros((ny, nz), jnp.float32)
        tau, rho = lax.fori_loop(0, bands, body, (zero, zero))
        lt[0, x] = 0.5 * tau
        lt[1, x] = rho + first * core[x]
        return 0

    lax.fori_loop(0, nx, sums_x, 0)

    def piece(m):
        return (pl.ds(lax.div(m, G) * px, px), pl.ds(pl.multiple_of(lax.rem(m, G) * R, 8), R))

    lgot = []
    for k in range(1, NB):
        xs, ys = piece(bpeer(k))
        lgot.append(remote(lt.at[:, xs, ys, :], lred.at[k], ls.at[k], lr.at[k], {"band": bpeer(k)}))
    xs, ys = piece(bi)
    total = lt[:, xs, ys, :]
    for k in range(1, NB):
        lgot[k - 1].wait_recv()
        total = total + lred[k]
    lsum[...] = total
    lmove = moved(lsum, lyz, ms, mr, ml, tg, tb)
    for c in range(1, CH):
        spreads.append(spread(c))

    ugot, rgot, rown = [], [], []

    def share(c, move):
        move()
        ugot.append([
            remote(lw.at[c, bi], lw.at[c, bi], us.at[c, k], ur.at[c, k], {"band": bpeer(k)})
            for k in range(1, NB)
        ])

    move = None
    for c in range(CH):
        got, own = spreads[c]
        own.wait()
        for copy in got:
            copy.wait_recv()

        def taux_body(b, acc):
            g = derive_lead(F[c, b])
            return acc + (0.5 * occ[b]) * (g * g)

        taux = lax.fori_loop(0, bands, taux_body, jnp.zeros((X, rc, nz), jnp.float32))
        for j in range(NB):
            part[c, j] = taux[j * px : (j + 1) * px]
        pgot = [
            remote(part.at[c, bpeer(k)], red.at[c, k], ps.at[c, k], pr.at[c, k], {"band": bpeer(k)})
            for k in range(1, NB)
        ]
        if c == 0:
            lmove()
        else:
            share(c - 1, move)
        kinetic = part[c, bi] + lyz[0, :, c * rc : (c + 1) * rc]
        density = lyz[1, :, c * rc : (c + 1) * rc]
        third = jnp.exp(jnp.log(density) * (1.0 / 3.0))
        uniform = 2.871 * (density * third * third)
        for k in range(1, NB):
            pgot[k - 1].wait_recv()
            kinetic = kinetic + red[c, k]
        ratio = kinetic / (kinetic + uniform)
        wy[c, bi] = 1.0 + 0.4 * ratio
        wgot = [
            remote(wy.at[c, bi], wy.at[c, bi], ws.at[c, k], wr.at[c, k], {"band": bpeer(k)})
            for k in range(1, NB)
        ]
        wv[c, 0] = 1.0 + 0.4 * ratio
        wv[c, 1] = -0.7386 * third * (1.0 + 0.3 * ratio)
        move = moved(wv.at[c], lw.at[c, sb], vs.at[c], vr.at[c], vl.at[c], sg, sb)
        for copy in wgot:
            copy.wait_recv()
        weight = jnp.concatenate([wy[c, j] for j in range(NB)], axis=0)

        def dx_body(b, _):
            dx[c, b] = -0.5 * derive_lead(weight * derive_lead(F[c, b]))
            return 0

        lax.fori_loop(0, bands, dx_body, 0)
        rgot.append([
            remote(dx.at[c, :, pl.ds(gpeer(k) * nx, nx)], ret.at[c, me], rs.at[c, k], rr.at[c, k], {"grid": gpeer(k)})
            for k in range(1, G)
        ])
        rown.append(local(dx.at[c, :, mine], ret.at[c, me], ro.at[c]))
    share(CH - 1, move)

    for c in range(CH):
        for copy in ugot[c]:
            copy.wait_recv()
        for m in range(NB):
            i, at = (m // G) * px, (m % G) * R + c * rc
            wl[0, i : i + px, at : at + rc] = lw[c, m, 0]
            wl[1, i : i + px, at : at + rc] = lw[c, m, 1] + lpot[i : i + px, at : at + rc]

    def apply_x(x, _):
        w = wl[0, x]
        v = wl[1, x]

        def body(b, _):
            div = derive_tile(w * gys[b, x], 0) + derive_tile(w * gzs[b, x], 1)
            out[b, x] = v * orb[b, x] - 0.5 * div
            return 0

        return lax.fori_loop(0, bands, body, 0)

    lax.fori_loop(0, nx, apply_x, 0)

    for c in range(CH):
        rown[c].wait()
        for copy in rgot[c]:
            copy.wait_recv()

        def add_body(b, _):
            for p in range(G):
                at = p * R + c * rc
                out[b, :, at : at + rc] = out[b, :, at : at + rc] + ret[c, p, b]
            return 0

        lax.fori_loop(0, bands, add_body, 0)
    for copy in sends:
        copy.wait_send()


def per_device(orbitals, occupation, core_density, local_potential):
    G = lax.axis_size("grid")
    NB = lax.axis_size("band")
    bands, nx, ny, nz = orbitals.shape
    X = nx * G
    R = ny // G
    CH = 2 if R % 16 == 0 else 1
    rc = R // CH
    px = X // NB
    f32 = jnp.float32
    dma = pltpu.SemaphoreType.DMA
    vmem = pl.BlockSpec(memory_space=pltpu.VMEM)
    return pl.pallas_call(
        functools.partial(kernel, G, NB, CH),
        out_shape=jax.ShapeDtypeStruct(orbitals.shape, f32),
        in_specs=[pl.BlockSpec(memory_space=pltpu.HBM)] * 4,
        out_specs=vmem,
        scratch_shapes=[
            pltpu.VMEM((bands, nx, ny, nz), f32),
            pltpu.SMEM((bands,), f32),
            pltpu.VMEM((nx, ny, nz), f32),
            pltpu.VMEM((nx, ny, nz), f32),
            pltpu.VMEM((CH, bands, X, rc, nz), f32),
            pltpu.VMEM((2, nx, ny, nz), f32),
            pltpu.VMEM((NB, 2, px, R, nz), f32),
            pltpu.VMEM((2, px, R, nz), f32),
            pltpu.VMEM((2, px, R, nz), f32),
            pltpu.VMEM((CH, NB, px, rc, nz), f32),
            pltpu.VMEM((CH, NB, px, rc, nz), f32),
            pltpu.VMEM((CH, 2, px, rc, nz), f32),
            pltpu.VMEM((CH, NB, px, rc, nz), f32),
            pltpu.VMEM((CH, NB, 2, px, rc, nz), f32),
            pltpu.VMEM((2, nx, ny, nz), f32),
            pltpu.VMEM((CH, bands, X, rc, nz), f32),
            pltpu.VMEM((CH, G, bands, nx, rc, nz), f32),
            pltpu.VMEM((bands, nx, ny, nz), f32),
            pltpu.VMEM((bands, nx, ny, nz), f32),
            dma((4,)), dma((CH, G)), dma((CH, G)), dma((CH,)),
            dma((NB,)), dma((NB,)), dma, dma, dma,
            dma((CH, NB)), dma((CH, NB)),
            dma((CH, NB)), dma((CH, NB)),
            dma((CH,)), dma((CH,)), dma((CH,)),
            dma((CH, NB)), dma((CH, NB)),
            dma((CH, G)), dma((CH, G)), dma((CH,)),
        ],
        compiler_params=pltpu.CompilerParams(
            collective_id=0, has_side_effects=True, vmem_limit_bytes=26 * 1024 * 1024
        ),
    )(*(
        pltpu.with_memory_space_constraint(a, pltpu.HBM)
        for a in (orbitals, occupation, core_density, local_potential)
    ))


def solution(mesh):
    in_specs = (
        P("band", "grid", None, None),
        P("band"),
        P("grid", None, None),
        P("grid", None, None),
    )
    out_specs = P("band", "grid", None, None)
    return jax.shard_map(
        per_device, mesh=mesh, in_specs=in_specs, out_specs=out_specs, check_vma=False
    )
```

time: 81.3 us -> 69.3 us (0.85)
  Pallas kernels: 77.5 us -> 67.7 us
  local copies, waits for them, and re-layouts: 3.56 us -> 1.49 us
    pallas_call x1, Pallas kernels: 77.5 us -> 67.7 us  [per_device(): pl.pallas_call(functools.partial(kernel, G, NB, CH), out_shape=jax.ShapeD...]
    unnamed x1, local copies, waits for them, and re-layouts: 3.56 us -> 1.49 us
where the time goes in v2:
time: 69.3 us; the launch traced here: 69.2 us
  Pallas kernels  67.7 us (98%)
  local copies, waits for them, and re-layouts  1.49 us (2%)
    pallas_call x1, Pallas kernels, per_device(): pl.pallas_call(functools.partial(kernel, G, NB, CH), out_shape=jax.ShapeD...  67.7 us
    unnamed x1, local copies, waits for them, and re-layouts  1.49 us

profile of v2, /device:TPU:0, one launch (start us, length us, event | category | flops | bytes accessed | tf_op | source)
XLA Modules:
  0.0 69.2 jit_solution(11529398067605107786)
XLA Ops:
  0.0 67.7 %shard_map.46 = f32[20,4,64,128]{3,2,1,0:T(8,128)S(1)} custom-call(f32[20,4,64,128]{3,2,1,0:T(8,128)} %orb_hbm.1, f32[20]{0:T(128)} %occ_hbm.1, f32[4,64,128]{2,1,0:T(8,128)} %core_hbm.1, f32[4,64,128]{2,1,0:T(8,128)} %lpot_hbm.1), custom_call_target="tpu_custom_call" | custom-call | tf_op jit(solution)/shard_map/pallas_call | solution.py:276
  67.7 1.5 %copy.6 = f32[20,4,64,128]{3,2,1,0:T(8,128)} copy(f32[20,4,64,128]{3,2,1,0:T(8,128)S(1)} %shard_map.46) | data formatting | bytes 5242880

commit v3 on v2

--- a/solution.py
+++ b/solution.py
@@ -137,7 +137,7 @@
             return tau + o * (gy * gy + gz * gz), rho + o * (f * f)
 
         zero = jnp.zeros((ny, nz), jnp.float32)
-        tau, rho = lax.fori_loop(0, bands, body, (zero, zero))
+        tau, rho = lax.fori_loop(0, bands, body, (zero, zero), unroll=2)
         lt[0, x] = 0.5 * tau
         lt[1, x] = rho + first * core[x]
         return 0

time: 69.3 us -> 68.3 us (0.986)
  Pallas kernels: 67.7 us -> 66.7 us
    pallas_call x1, Pallas kernels: 67.7 us -> 66.7 us  [per_device(): pl.pallas_call(functools.partial(kernel, G, NB, CH), out_shape=jax.ShapeD...]
where the time goes in v3:
time: 68.3 us; the launch traced here: 68.2 us
  Pallas kernels  66.7 us (98%)
  local copies, waits for them, and re-layouts  1.49 us (2%)
    pallas_call x1, Pallas kernels, per_device(): pl.pallas_call(functools.partial(kernel, G, NB, CH), out_shape=jax.ShapeD...  66.7 us
    unnamed x1, local copies, waits for them, and re-layouts  1.49 us

profile of v3, /device:TPU:0, one launch (start us, length us, event | category | flops | bytes accessed | tf_op | source)
XLA Modules:
  0.0 68.2 jit_solution(7535229724448998699)
XLA Ops:
  0.0 66.7 %shard_map.46 = f32[20,4,64,128]{3,2,1,0:T(8,128)S(1)} custom-call(f32[20,4,64,128]{3,2,1,0:T(8,128)} %orb_hbm.1, f32[20]{0:T(128)} %occ_hbm.1, f32[4,64,128]{2,1,0:T(8,128)} %core_hbm.1, f32[4,64,128]{2,1,0:T(8,128)} %lpot_hbm.1), custom_call_target="tpu_custom_call" | custom-call | tf_op jit(solution)/shard_map/pallas_call | solution.py:276
  66.7 1.5 %copy.6 = f32[20,4,64,128]{3,2,1,0:T(8,128)} copy(f32[20,4,64,128]{3,2,1,0:T(8,128)S(1)} %shard_map.46) | data formatting | bytes 5242880
